TPU v7x, 32 devices: a whole 2x2x4 slice. The times are simulated.
32 devices in a mesh: leaf: 32 (over z, y, x, core).
Axes of the slice: x: 2, y: 2, z: 4, core: 2. Of those that a mesh axis runs over, the one named last changes fastest.
Arguments:
- points: bfloat16 [65536, 128], P('leaf'), may hold values from -6 to 6
- charges: bfloat16 [65536, 256], P('leaf'), may hold values from -6 to 6
- order: int32 [32, 2048], P('leaf'), may hold values from 0 to 2047, each once within a row
- near: int32 [32, 2], P('leaf'), may hold values from 0 to 31, as said below
- bases: bfloat16 [65536, 256], P('leaf'), may hold values from -0.125 to 0.125
- lift_leaf: float32 [8192, 256], P('leaf'), may hold values from -0.1875 to 0.1875
- lift_node: float32 [2048, 256], P('leaf'), may hold values from -0.1875 to 0.1875
- proxy_leaf: float32 [8192, 128], P('leaf'), may hold values from -5 to 5
- proxy_node: float32 [2048, 128], P('leaf'), may hold values from -5 to 5
- proxy_top: float32 [512, 128], P('leaf'), may hold values from -5 to 5
Outputs:
- potential: bfloat16 [65536, 256], P('leaf')
Inputs may be any that keep to these rules, and one draw needn't show every extreme that they name: `order`: each row is a permutation of the leaf's 2048 positions. `near`: row l names two distinct leaves other than l from l's aligned group of four leaves; the relation is symmetric, and the group's remaining leaf is l's far partner, whose index differs from l in exactly one of the two lowest bits.
All inputs are finite; a program needn't handle non-finite values.
Results may differ from a plain program's by a relative error of at most 0.0049.
Values may be sent and summed in bfloat16 or wider, within the bound.
A program may use at most 64 MiB of HBM per device.

v0:
```python
import jax
import jax.numpy as jnp
from jax import lax
from jax.sharding import PartitionSpec as P

D = 128
NRHS = 256
RANK = 256
LEAF = 2048


highest = lax.Precision.HIGHEST


def from_partner(shard, axis, stride):
    return lax.ppermute(shard, axis, [(i, i ^ 1 << stride) for i in range(lax.axis_size(axis))])


def couple(left, right):
    products = jnp.dot(left, right.T, precision=highest)
    left_norm = jnp.sum(left * left, axis=1)
    right_norm = jnp.sum(right * right, axis=1)
    return jnp.exp((2.0 * products - left_norm[:, None] - right_norm[None, :]) * (2.0 / D))


def near_term(own, other, values):
    block_rows = min(512, LEAF)
    other_norm = jnp.sum(jnp.square(other.astype(jnp.float32)), axis=1)

    def one_block(row_points):
        products = jnp.dot(row_points, other.T, preferred_element_type=jnp.float32)
        row_norm = jnp.sum(jnp.square(row_points.astype(jnp.float32)), axis=1)
        tile = jnp.exp((2.0 * products - row_norm[:, None] - other_norm[None, :]) * (2.0 / D))
        return jnp.dot(tile.astype(jnp.bfloat16), values, preferred_element_type=jnp.float32)

    blocks = lax.map(one_block, own.reshape(LEAF // block_rows, block_rows, D))
    return blocks.reshape(LEAF, NRHS)


def group_collect(pieces, low_bit, position):
    partner = from_partner(pieces, "leaf", low_bit)
    low_value = position // 2**low_bit % 2
    pairs = tuple(
        (
            jnp.where(low_value == 0, jnp.stack([mine, other]), jnp.stack([other, mine]))
            for mine, other in zip(pieces, partner)
        )
    )
    partner_pairs = from_partner(pairs, "leaf", low_bit + 1)
    high_value = position // 2 ** (low_bit + 1) % 2
    return tuple(
        (
            jnp.where(
                high_value == 0,
                jnp.concatenate([mine, other], 0),
                jnp.concatenate([other, mine], 0),
            )
            for mine, other in zip(pairs, partner_pairs)
        )
    )


def pick_sibling(relation, near_one, near_two, near_three):
    chosen_points = jnp.where(
        relation == 1, near_one[0], jnp.where(relation == 2, near_two[0], near_three[0])
    )
    chosen_rhs = jnp.where(
        relation == 1, near_one[1], jnp.where(relation == 2, near_two[1], near_three[1])
    )
    return (chosen_points, chosen_rhs)


def per_device(
    points, charges, order, near, bases, lift_leaf, lift_node, proxy_leaf, proxy_node, proxy_top
):
    leaf_index = lax.axis_index("leaf")
    leaf_slot = leaf_index % 4
    group_slot = leaf_index // 4 % 4
    top_part = leaf_index % 16
    top_nodes = lax.axis_size("leaf") // 16
    own_node = leaf_index // 16
    rhs = jnp.take(charges, order[0], axis=0)
    near_one = from_partner((points, rhs), "leaf", 0)
    near_two = from_partner((points, rhs), "leaf", 1)
    near_three = from_partner((near_two[0], near_two[1]), "leaf", 0)
    coefficient = lax.dot_general(
        bases, rhs, (((0,), (0,)), ((), ())), preferred_element_type=jnp.float32
    )
    up_term = lax.dot_general(lift_leaf, coefficient, (((0,), (0,)), ((), ())), precision=highest)
    own_block = jnp.concatenate([coefficient, proxy_leaf], 1)
    total = near_term(points, points, rhs)
    for column in range(2):
        relation = jnp.bitwise_xor(near[0, column] % 4, leaf_slot)
        chosen_points, chosen_rhs = pick_sibling(relation, near_one, near_two, near_three)
        total = total + near_term(points, chosen_points, chosen_rhs)
    first_quad = group_collect((own_block, up_term, proxy_node, lift_node), 0, leaf_index)
    leaf_data = first_quad[0].reshape(4 * RANK, NRHS + D)
    node_coeff = jnp.sum(first_quad[1], axis=0)
    node_proxy = first_quad[2].reshape(RANK, D)
    node_lift = first_quad[3].reshape(RANK, RANK)
    top_term = lax.dot_general(node_lift, node_coeff, (((0,), (0,)), ((), ())), precision=highest)
    node_block = jnp.concatenate([node_coeff, node_proxy], 1)
    top_rows = RANK // 16
    second_quad = group_collect((node_block, top_term), 2, leaf_index)
    group_data = second_quad[0].reshape(4 * RANK, NRHS + D)
    top_coeff = jnp.sum(second_quad[1], axis=0)
    top_piece = jnp.concatenate(
        [lax.dynamic_slice_in_dim(top_coeff, top_part * top_rows, top_rows, 0), proxy_top], 1
    )
    top_all = lax.all_gather(top_piece, "leaf", axis=0, tiled=True)
    owner = jnp.arange(top_nodes * RANK, dtype=jnp.int32) // RANK
    top_proxy_all = top_all[:, NRHS:]
    own_top_proxy = lax.dynamic_slice_in_dim(top_proxy_all, own_node * RANK, RANK, 0)
    top_kernel = jnp.where(owner[None, :] != own_node, couple(own_top_proxy, top_proxy_all), 0.0)
    field_top = jnp.dot(top_kernel, top_all[:, :NRHS], precision=highest)
    sibling_owner = jnp.arange(4 * RANK, dtype=jnp.int32) // RANK
    node_kernel = jnp.where(
        sibling_owner[None, :] != group_slot, couple(node_proxy, group_data[:, NRHS:]), 0.0
    )
    field_node = jnp.dot(node_kernel, group_data[:, :NRHS], precision=highest)
    field_node = field_node + jnp.dot(node_lift, field_top, precision=highest)
    partner = 6 - leaf_slot - near[0, 0] % 4 - near[0, 1] % 4
    leaf_kernel = jnp.where(
        sibling_owner[None, :] == partner, couple(proxy_leaf, leaf_data[:, NRHS:]), 0.0
    )
    field_leaf = jnp.dot(leaf_kernel, leaf_data[:, :NRHS], precision=highest)
    field_leaf = (field_leaf + jnp.dot(lift_leaf, field_node, precision=highest)).astype(
        jnp.bfloat16
    )
    descent = jnp.dot(bases, field_leaf, preferred_element_type=jnp.float32)
    return (total + descent).astype(jnp.bfloat16)


def solution(mesh):
    return jax.shard_map(
        per_device,
        mesh=mesh,
        in_specs=(
            P("leaf", None),
            P("leaf", None),
            P("leaf", None),
            P("leaf", None),
            P("leaf", None),
            P("leaf", None),
            P("leaf", None),
            P("leaf", None),
            P("leaf", None),
            P("leaf", None),
        ),
        out_specs=P("leaf", None),
        check_vma=False,
    )
```

profile of v0, /device:TPU:0, one launch (start us, length us, event | category | flops | bytes accessed | tf_op | source)
XLA Modules:
  0.0 207.7 jit_solution(7059513540064207651)
XLA Ops:
  1.5 8.0 %gather_fusion = bf16[2048,256]{1,0:T(8,128)(2,1)S(1)} fusion(bf16[2048,256]{1,0:T(8,128)(2,1)} %param.17, s32[2048]{0:T(1024)S(1)} %broadcast_clamp_fusion), kind=kCustom, calls=%fused_computation | custom fusion | bytes 2105344 | tf_op jit(solution)/shard_map/jit(_take)/gather | solution.py:82
  10.8 3.0 %collective-permute-start.4 = (bf16[2048,256]{1,0:T(8,128)(2,1)}, bf16[2048,256]{1,0:T(8,128)(2,1)}, u32[]{:S(2)}, u32[]{:S(2)}) collective-permute-start(bf16[2048,256]{1,0:T(8,128)(2,1)} %broadcast_select_fusion), channel_id=1, source_target_pairs={{0,2},{1,3},{2,0},{3,1},{4,6},{5,7},{6,4},{7,5},{8,10},{9,11},{10,... | collective-permute-start | bytes 3145736 | tf_op jit(solution)/shard_map/ppermute | solution.py:16
  13.7 1.7 fusion.77
  21.5 1.4 multiply_reduce_fusion.5
  23.0 15.5 %while.30 = (s32[]{:T(128)}, f32[4,512,256]{2,1,0:T(8,128)S(1)}, bf16[4,512,128]{2,1,0:T(8,128)(2,1)}, bf16[2048,128]{1,0:T(8,128)(2,1)}, f32[2048]{0:T(1024)S(1)}, /*index=5*/bf16[2048,256]{1,0:T(8,128)(2,1)}, s32[]{:T(128)}) while((s32[]{:T(128)}, f32[4,512,256]{2,1,0:T(8,128)S(1)}, bf16[4,512,128]{2,1,0:T(8,128)(2,1)}, ...), condition=%wide.region_3.4_spmd, body=%wide.region_1.3_spmd.sunk | while | flops 810745344 | bytes 2372689 | solution.py:36
  24.1 2.8 %fusion.120 = f32[4,512,256]{2,1,0:T(8,128)S(1)} fusion(f32[4,512,256]{2,1,0:T(8,128)S(1)} %get-tuple-element.298, s32[]{:T(128)} %get-tuple-element.297, bf16[2048,256]{1,0:T(8,128)(2,1)} %get-tuple-element.309, bf16[2048,128]{1,0:T(8,128)(2,1)} %get-tuple-element.307, f32[2048]{0:T(1024)S(1)} %get-tuple-element.308, ...), kind=kOutput, calls=%fused_computation.4.clone.1 | convolution fusion | flops 810549248 | bytes 2239488 | tf_op jit(solution)/shard_map/while/body/eval_jaxpr/dot_general | solution.py:34
  28.0 2.8 %fusion.120 = f32[4,512,256]{2,1,0:T(8,128)S(1)} fusion(f32[4,512,256]{2,1,0:T(8,128)S(1)} %get-tuple-element.298, s32[]{:T(128)} %get-tuple-element.297, bf16[2048,256]{1,0:T(8,128)(2,1)} %get-tuple-element.309, bf16[2048,128]{1,0:T(8,128)(2,1)} %get-tuple-element.307, f32[2048]{0:T(1024)S(1)} %get-tuple-element.308, ...), kind=kOutput, calls=%fused_computation.4.clone.1 | convolution fusion | flops 810549248 | bytes 2239488 | tf_op jit(solution)/shard_map/while/body/eval_jaxpr/dot_general | solution.py:34
  31.9 2.8 %fusion.120 = f32[4,512,256]{2,1,0:T(8,128)S(1)} fusion(f32[4,512,256]{2,1,0:T(8,128)S(1)} %get-tuple-element.298, s32[]{:T(128)} %get-tuple-element.297, bf16[2048,256]{1,0:T(8,128)(2,1)} %get-tuple-element.309, bf16[2048,128]{1,0:T(8,128)(2,1)} %get-tuple-element.307, f32[2048]{0:T(1024)S(1)} %get-tuple-element.308, ...), kind=kOutput, calls=%fused_computation.4.clone.1 | convolution fusion | flops 810549248 | bytes 2239488 | tf_op jit(solution)/shard_map/while/body/eval_jaxpr/dot_general | solution.py:34
  35.7 2.8 %fusion.120 = f32[4,512,256]{2,1,0:T(8,128)S(1)} fusion(f32[4,512,256]{2,1,0:T(8,128)S(1)} %get-tuple-element.298, s32[]{:T(128)} %get-tuple-element.297, bf16[2048,256]{1,0:T(8,128)(2,1)} %get-tuple-element.309, bf16[2048,128]{1,0:T(8,128)(2,1)} %get-tuple-element.307, f32[2048]{0:T(1024)S(1)} %get-tuple-element.308, ...), kind=kOutput, calls=%fused_computation.4.clone.1 | convolution fusion | flops 810549248 | bytes 2239488 | tf_op jit(solution)/shard_map/while/body/eval_jaxpr/dot_general | solution.py:34
  40.3 1.6 multiply_reduce_fusion.11
  42.9 2.0 maximum_select_fusion.6
  44.9 2.0 collective-permute-start.11
  49.9 12.4 %collective-permute-done.15 = f32[2,64,256]{2,1,0:T(8,128)S(1)} collective-permute-done((f32[2,64,256]{2,1,0:T(8,128)S(1)}, f32[2,64,256]{2,1,0:T(8,128)S(1)}, u32[]{:S(2)}, u32[]{:S(2)}) %collective-permute-start.15) | collective-permute-done | bytes 131104 | tf_op jit(solution)/shard_map/ppermute | solution.py:16
  62.4 1.8 collective-permute-start.9
  64.5 1.7 fusion.57
  66.8 1.6 collective-permute-start.16
  71.7 3.8 %collective-permute-done.16 = f32[256,256]{1,0:T(8,128)} collective-permute-done((f32[256,256]{1,0:T(8,128)S(1)}, f32[256,256]{1,0:T(8,128)}, u32[]{:S(2)}, u32[]{:S(2)}) %collective-permute-start.16) | collective-permute-done | bytes 262176 | tf_op jit(solution)/shard_map/ppermute | solution.py:16
  75.4 1.5 collective-permute-start.12
  77.0 1.9 maximum_select_fusion.7
  78.9 1.6 collective-permute-start.17
  80.7 2.9 %multiply_reduce_fusion.4 = (f32[2048]{0:T(1024)S(1)}, bf16[2048,128]{1,0:T(8,128)(2,1)}, f32[2048]{0:T(1024)S(1)}, bf16[2048,128]{1,0:T(8,128)(2,1)}) fusion(bf16[2048,128]{1,0:T(8,128)(2,1)} %collective-permute-done, bf16[2048,128]{1,0:T(8,128)(2,1)} %collective-permute-done.1, bf16[2048,128]{1,0:T(8,128)(2,1)} %collective-permute-done.2, pred[]{:T(512)S(6)} %eq.60, ...), kind=kLoop, calls=%fused_computation.69 | loop fusion | flops 2617344 | bytes 2637828 | tf_op jit(solution)/shard_map/reduce_sum | solution.py:28
  83.6 2.3 %collective-permute-done.12 = f32[256,384]{0,1:T(8,128)S(1)} collective-permute-done((f32[256,384]{0,1:T(8,128)S(1)}, f32[256,384]{0,1:T(8,128)S(1)}, u32[]{:S(2)}, u32[]{:S(2)}) %collective-permute-start.12) | collective-permute-done | bytes 393248 | tf_op jit(solution)/shard_map/ppermute | solution.py:16
  85.9 1.6 collective-permute-start.13
  87.6 1.6 collective-permute-done.7
  89.2 2.7 %maximum_select_fusion = f32[4,256,384]{1,2,0:T(8,128)} fusion(f32[2,256,384]{1,2,0:T(8,128)} %collective-permute-done.7, f32[2,256,384]{1,2,0:T(8,128)S(1)} %maximum_select_fusion.4, pred[]{:T(512)S(6)} %eq.65), kind=kLoop, calls=%fused_computation.35 | loop fusion | flops 1179648 | bytes 3145729 | tf_op jit(solution)/shard_map/jit(_where)/select_n | solution.py:53
  91.9 1.9 copy.33
  94.0 2.8 %fusion.44 = f32[1024,256]{1,0:T(8,128)} fusion(f32[256,128]{1,0:T(8,128)S(1)} %copy-done.10, f32[1024]{0:T(1024)S(1)} %multiply_reduce_fusion.7, f32[256]{0:T(256)} %multiply_reduce_fusion.11, pred[1024]{0:T(1024)(128)(4,1)} %fusion.67, f32[1024,384]{1,0:T(8,128)S(1)} %bitcast.120), kind=kOutput, calls=%fused_computation.48 | convolution fusion | flops 403963904 | bytes 1710080 | tf_op jit(solution)/shard_map/dot_general | solution.py:20
  96.9 1.7 fusion.58
  98.6 47.8 %all_gather.3 = f32[512,384]{1,0:T(8,128)S(1)} all-gather(f32[16,384]{1,0:T(8,128)S(1)} %pad_maximum_fusion.2), channel_id=1, replica_groups=mesh['leaf'=32] {'leaf'}, dimensions={0}, use_global_device_ids=true | all-gather | bytes 811008 | tf_op jit(solution)/shard_map/all_gather | solution.py:110
  149.1 2.7 %maximum_select_fusion.1 = f32[4,256,384]{1,2,0:T(8,128)} fusion(f32[2,256,384]{1,2,0:T(8,128)} %collective-permute-done.13, f32[2,256,384]{1,2,0:T(8,128)S(1)} %maximum_select_fusion.5, pred[]{:T(512)S(6)} %eq.67), kind=kLoop, calls=%fused_computation.36 | loop fusion | flops 1179648 | bytes 3145729 | tf_op jit(solution)/shard_map/jit(_where)/select_n | solution.py:53
  151.8 3.1 %copy.35 = f32[4,256,384]{2,1,0:T(8,128)} copy(f32[4,256,384]{1,2,0:T(8,128)} %maximum_select_fusion.1) | data formatting | bytes 3145728 | tf_op jit(solution)/shard_map/jit(_where)/select_n | solution.py:53
  156.3 2.3 %fusion.39 = f32[256,1024]{1,0:T(8,128)S(1)} fusion(f32[256,128]{1,0:T(8,128)S(1)} %bitcast.130, f32[1024]{0:T(1024)S(1)} %multiply_reduce_fusion.6, f32[256]{0:T(256)S(1)} %copy-done.15, pred[1024]{0:T(1024)(128)(4,1)S(1)} %copy-done.16, f32[1024,384]{1,0:T(8,128)} %bitcast.123), kind=kOutput, calls=%fused_computation.42 | convolution fusion | flops 403963904 | bytes 1710080 | tf_op jit(solution)/shard_map/dot_general | solution.py:20
  160.0 1.8 fusion.50
  161.9 3.4 %select_select_fusion.1 = (bf16[2048,256]{1,0:T(8,128)(2,1)}, bf16[2048,256]{1,0:T(8,128)(2,1)}) fusion(bf16[2048,256]{1,0:T(8,128)(2,1)} %collective-permute-done.3, bf16[2048,256]{1,0:T(8,128)(2,1)} %collective-permute-done.4, bf16[2048,256]{1,0:T(8,128)(2,1)} %collective-permute-done.5, pred[]{:T(512)S(6)} %eq.60, pred[]{:T(512)S(6)} %eq.59, pred[]{:T(512)S(6)} %eq.62, ...), kind=kLoop, calls=%fused_computation.68 | loop fusion | flops 2097152 | bytes 5242884 | tf_op jit(solution)/shard_map/jit(_where)/select_n | solution.py:67
  165.4 15.7 %while.31 = (s32[]{:T(128)}, f32[4,512,256]{2,1,0:T(8,128)S(1)}, bf16[4,512,128]{2,1,0:T(8,128)(2,1)}, bf16[2048,128]{1,0:T(8,128)(2,1)}, f32[2048]{0:T(1024)S(1)}, /*index=5*/bf16[2048,256]{1,0:T(8,128)(2,1)}, s32[]{:T(128)}) while((s32[]{:T(128)}, f32[4,512,256]{2,1,0:T(8,128)S(1)}, bf16[4,512,128]{2,1,0:T(8,128)(2,1)}, ...), condition=%wide.region_7.8_spmd, body=%wide.region_5.7_spmd.sunk | while | flops 810745344 | bytes 2372689 | solution.py:36
  166.7 2.8 %fusion.124 = f32[4,512,256]{2,1,0:T(8,128)S(1)} fusion(f32[4,512,256]{2,1,0:T(8,128)S(1)} %get-tuple-element.319, s32[]{:T(128)} %get-tuple-element.318, bf16[2048,256]{1,0:T(8,128)(2,1)} %get-tuple-element.330, bf16[2048,128]{1,0:T(8,128)(2,1)} %get-tuple-element.328, f32[2048]{0:T(1024)S(1)} %get-tuple-element.329, ...), kind=kOutput, calls=%fused_computation.14.clone.1 | convolution fusion | flops 810549248 | bytes 2239488 | tf_op jit(solution)/shard_map/while/body/eval_jaxpr/dot_general | solution.py:34
  170.5 2.8 %fusion.124 = f32[4,512,256]{2,1,0:T(8,128)S(1)} fusion(f32[4,512,256]{2,1,0:T(8,128)S(1)} %get-tuple-element.319, s32[]{:T(128)} %get-tuple-element.318, bf16[2048,256]{1,0:T(8,128)(2,1)} %get-tuple-element.330, bf16[2048,128]{1,0:T(8,128)(2,1)} %get-tuple-element.328, f32[2048]{0:T(1024)S(1)} %get-tuple-element.329, ...), kind=kOutput, calls=%fused_computation.14.clone.1 | convolution fusion | flops 810549248 | bytes 2239488 | tf_op jit(solution)/shard_map/while/body/eval_jaxpr/dot_general | solution.py:34
  174.4 2.8 %fusion.124 = f32[4,512,256]{2,1,0:T(8,128)S(1)} fusion(f32[4,512,256]{2,1,0:T(8,128)S(1)} %get-tuple-element.319, s32[]{:T(128)} %get-tuple-element.318, bf16[2048,256]{1,0:T(8,128)(2,1)} %get-tuple-element.330, bf16[2048,128]{1,0:T(8,128)(2,1)} %get-tuple-element.328, f32[2048]{0:T(1024)S(1)} %get-tuple-element.329, ...), kind=kOutput, calls=%fused_computation.14.clone.1 | convolution fusion | flops 810549248 | bytes 2239488 | tf_op jit(solution)/shard_map/while/body/eval_jaxpr/dot_general | solution.py:34
  178.3 2.8 %fusion.124 = f32[4,512,256]{2,1,0:T(8,128)S(1)} fusion(f32[4,512,256]{2,1,0:T(8,128)S(1)} %get-tuple-element.319, s32[]{:T(128)} %get-tuple-element.318, bf16[2048,256]{1,0:T(8,128)(2,1)} %get-tuple-element.330, bf16[2048,128]{1,0:T(8,128)(2,1)} %get-tuple-element.328, f32[2048]{0:T(1024)S(1)} %get-tuple-element.329, ...), kind=kOutput, calls=%fused_computation.14.clone.1 | convolution fusion | flops 810549248 | bytes 2239488 | tf_op jit(solution)/shard_map/while/body/eval_jaxpr/dot_general | solution.py:34
  182.6 15.5 %while.32 = (s32[]{:T(128)}, f32[4,512,256]{2,1,0:T(8,128)S(1)}, bf16[4,512,128]{2,1,0:T(8,128)(2,1)}, bf16[2048,128]{1,0:T(8,128)(2,1)}, f32[2048]{0:T(1024)S(1)}, /*index=5*/bf16[2048,256]{1,0:T(8,128)(2,1)}, s32[]{:T(128)}) while((s32[]{:T(128)}, f32[4,512,256]{2,1,0:T(8,128)S(1)}, bf16[4,512,128]{2,1,0:T(8,128)(2,1)}, ...), condition=%wide.region_11.12_spmd, body=%wide.region_9.11_spmd.sunk | while | flops 810745344 | bytes 2372689 | solution.py:36
  183.6 2.8 %fusion.128 = f32[4,512,256]{2,1,0:T(8,128)S(1)} fusion(f32[4,512,256]{2,1,0:T(8,128)S(1)} %get-tuple-element.277, s32[]{:T(128)} %get-tuple-element.276, bf16[2048,256]{1,0:T(8,128)(2,1)} %get-tuple-element.288, bf16[2048,128]{1,0:T(8,128)(2,1)} %get-tuple-element.286, f32[2048]{0:T(1024)S(1)} %get-tuple-element.287, ...), kind=kOutput, calls=%fused_computation.24.clone.1 | convolution fusion | flops 810549248 | bytes 2239488 | tf_op jit(solution)/shard_map/while/body/eval_jaxpr/dot_general | solution.py:34
  187.5 2.8 %fusion.128 = f32[4,512,256]{2,1,0:T(8,128)S(1)} fusion(f32[4,512,256]{2,1,0:T(8,128)S(1)} %get-tuple-element.277, s32[]{:T(128)} %get-tuple-element.276, bf16[2048,256]{1,0:T(8,128)(2,1)} %get-tuple-element.288, bf16[2048,128]{1,0:T(8,128)(2,1)} %get-tuple-element.286, f32[2048]{0:T(1024)S(1)} %get-tuple-element.287, ...), kind=kOutput, calls=%fused_computation.24.clone.1 | convolution fusion | flops 810549248 | bytes 2239488 | tf_op jit(solution)/shard_map/while/body/eval_jaxpr/dot_general | solution.py:34
  191.4 2.8 %fusion.128 = f32[4,512,256]{2,1,0:T(8,128)S(1)} fusion(f32[4,512,256]{2,1,0:T(8,128)S(1)} %get-tuple-element.277, s32[]{:T(128)} %get-tuple-element.276, bf16[2048,256]{1,0:T(8,128)(2,1)} %get-tuple-element.288, bf16[2048,128]{1,0:T(8,128)(2,1)} %get-tuple-element.286, f32[2048]{0:T(1024)S(1)} %get-tuple-element.287, ...), kind=kOutput, calls=%fused_computation.24.clone.1 | convolution fusion | flops 810549248 | bytes 2239488 | tf_op jit(solution)/shard_map/while/body/eval_jaxpr/dot_general | solution.py:34
  195.3 2.8 %fusion.128 = f32[4,512,256]{2,1,0:T(8,128)S(1)} fusion(f32[4,512,256]{2,1,0:T(8,128)S(1)} %get-tuple-element.277, s32[]{:T(128)} %get-tuple-element.276, bf16[2048,256]{1,0:T(8,128)(2,1)} %get-tuple-element.288, bf16[2048,128]{1,0:T(8,128)(2,1)} %get-tuple-element.286, f32[2048]{0:T(1024)S(1)} %get-tuple-element.287, ...), kind=kOutput, calls=%fused_computation.24.clone.1 | convolution fusion | flops 810549248 | bytes 2239488 | tf_op jit(solution)/shard_map/while/body/eval_jaxpr/dot_general | solution.py:34
  198.1 4.0 %add_add_fusion = f32[4,512,256]{2,1,0:T(8,128)} fusion(f32[4,512,256]{2,1,0:T(8,128)S(1)} %get-tuple-element.103, f32[4,512,256]{2,1,0:T(8,128)} %copy-done.1, f32[4,512,256]{2,1,0:T(8,128)} %copy-done.2), kind=kLoop, calls=%fused_computation.34 | loop fusion | flops 1048576 | bytes 8388608 | tf_op jit(solution)/shard_map/add | solution.py:95
  202.0 1.9 copy.39
  204.0 1.5 fusion.34
  205.4 2.3 %copy.37 = bf16[2048,256]{1,0:T(8,128)(2,1)} copy(bf16[2048,256]{0,1:T(8,128)(2,1)} %fusion.34) | data formatting | bytes 2097152 | tf_op jit(solution)/shard_map/convert_element_type | solution.py:131
  (108 shorter events, 35.0 us)
Async XLA Ops:
  0.0 13.7 %copy-start = (bf16[2048,256]{1,0:T(8,128)(2,1)S(1)}, bf16[2048,256]{1,0:T(8,128)(2,1)}, u32[]{:S(2)}) copy-start(bf16[2048,256]{1,0:T(8,128)(2,1)} %param.20) | copy-start | bytes 3145732
  9.5 5.9 %copy-start.6 = (f32[256,256]{1,0:T(8,128)S(1)}, f32[256,256]{1,0:T(8,128)}, u32[]{:S(2)}) copy-start(f32[256,256]{1,0:T(8,128)} %param.21) | copy-start | bytes 786436
  10.8 6.3 %copy-start.14 = (s32[1,2]{1,0:T(1,128)S(1)}, s32[1,2]{1,0:T(1,128)}, u32[]{:S(2)}) copy-start(s32[1,2]{1,0:T(1,128)} %param.19) | copy-start | bytes 28
  10.8 68.1 %collective-permute-start.4 = (bf16[2048,256]{1,0:T(8,128)(2,1)}, bf16[2048,256]{1,0:T(8,128)(2,1)}, u32[]{:S(2)}, u32[]{:S(2)}) collective-permute-start(bf16[2048,256]{1,0:T(8,128)(2,1)} %broadcast_select_fusion), channel_id=1, source_target_pairs={{0,2},{1,3},{2,0},{3,1},{4,6},{5,7},{6,4},{7,5},{8,10},{9,11},{10,... | collective-permute-start | bytes 3145736 | tf_op jit(solution)/shard_map/ppermute | solution.py:16
  16.6 26.3 %collective-permute-start.10 = (f32[256,256]{0,1:T(8,128)}, f32[256,256]{0,1:T(8,128)}, u32[]{:S(2)}, u32[]{:S(2)}) collective-permute-start(f32[256,256]{0,1:T(8,128)} %bitcast.20), channel_id=1, source_target_pairs={{0,1},{1,0},{2,3},{3,2},{4,5},{5,4},{6,7},{7,6},{8,9},{9,8},{10,11... | collective-permute-start | bytes 786440 | tf_op jit(solution)/shard_map/ppermute | solution.py:16
  16.6 32.5 %collective-permute-start.8 = (f32[64,128]{1,0:T(8,128)}, f32[64,128]{1,0:T(8,128)}, u32[]{:S(2)}, u32[]{:S(2)}) collective-permute-start(f32[64,128]{1,0:T(8,128)} %param.24), channel_id=1, source_target_pairs={{0,1},{1,0},{2,3},{3,2},{4,5},{5,4},{6,7},{7,6},{8,9},{9,8},{10,11... | collective-permute-start | bytes 98312 | tf_op jit(solution)/shard_map/ppermute | solution.py:16
  17.1 30.3 %collective-permute-start.14 = (f32[64,256]{1,0:T(8,128)}, f32[64,256]{1,0:T(8,128)}, u32[]{:S(2)}, u32[]{:S(2)}) collective-permute-start(f32[64,256]{1,0:T(8,128)} %param.22), channel_id=1, source_target_pairs={{0,1},{1,0},{2,3},{3,2},{4,5},{5,4},{6,7},{7,6},{8,9},{9,8},{10,11... | collective-permute-start | bytes 196616 | tf_op jit(solution)/shard_map/ppermute | solution.py:16
  17.1 45.3 %collective-permute-start.1 = (bf16[2048,128]{1,0:T(8,128)(2,1)}, bf16[2048,128]{1,0:T(8,128)(2,1)}, u32[]{:S(2)}, u32[]{:S(2)}) collective-permute-start(bf16[2048,128]{1,0:T(8,128)(2,1)} %param.16), channel_id=1, source_target_pairs={{0,2},{1,3},{2,0},{3,1},{4,6},{5,7},{6,4},{7,5},{8,10},{9,11},{10,... | collective-permute-start | bytes 1572872 | tf_op jit(solution)/shard_map/ppermute | solution.py:16
  38.6 27.6 %copy-start.1 = (f32[4,512,256]{2,1,0:T(8,128)}, f32[4,512,256]{2,1,0:T(8,128)S(1)}, u32[]{:S(2)}) copy-start(f32[4,512,256]{2,1,0:T(8,128)S(1)} %get-tuple-element.101) | copy-start | bytes 6291460
  44.9 19.3 %collective-permute-start.11 = (f32[2,256,256]{1,2,0:T(8,128)}, f32[2,256,256]{1,2,0:T(8,128)}, u32[]{:S(2)}, u32[]{:S(2)}) collective-permute-start(f32[2,256,256]{1,2,0:T(8,128)} %maximum_select_fusion.6), channel_id=1, source_target_pairs={{0,2},{1,3},{2,0},{3,1},{4,6},{5,7},{6,4},{7,5},{8,10},{9,11},{10,... | collective-permute-start | bytes 1572872 | tf_op jit(solution)/shard_map/ppermute | solution.py:16
  48.4 14.0 %collective-permute-start.15 = (f32[2,64,256]{2,1,0:T(8,128)S(1)}, f32[2,64,256]{2,1,0:T(8,128)S(1)}, u32[]{:S(2)}, u32[]{:S(2)}) collective-permute-start(f32[2,64,256]{2,1,0:T(8,128)S(1)} %maximum_select_fusion.10), channel_id=1, source_target_pairs={{0,2},{1,3},{2,0},{3,1},{4,6},{5,7},{6,4},{7,5},{8,10},{9,11},{10,... | collective-permute-start | bytes 393224 | tf_op jit(solution)/shard_map/ppermute | solution.py:16
  49.1 29.8 %collective-permute-start = (bf16[2048,128]{1,0:T(8,128)(2,1)}, bf16[2048,128]{1,0:T(8,128)(2,1)}, u32[]{:S(2)}, u32[]{:S(2)}) collective-permute-start(bf16[2048,128]{1,0:T(8,128)(2,1)} %param.16), channel_id=1, source_target_pairs={{0,1},{1,0},{2,3},{3,2},{4,5},{5,4},{6,7},{7,6},{8,9},{9,8},{10,11... | collective-permute-start | bytes 1572872 | tf_op jit(solution)/shard_map/ppermute | solution.py:16
  62.4 4.4 %collective-permute-start.6 = (f32[256,384]{0,1:T(8,128)}, f32[256,384]{0,1:T(8,128)S(1)}, u32[]{:S(2)}, u32[]{:S(2)}) collective-permute-start(f32[256,384]{0,1:T(8,128)} %get-tuple-element.153), channel_id=1, source_target_pairs={{0,1},{1,0},{2,3},{3,2},{4,5},{5,4},{6,7},{7,6},{8,9},{9,8},{10,11... | collective-permute-start | bytes 1179656 | tf_op jit(solution)/shard_map/ppermute | solution.py:16
  62.4 7.1 %copy-start.4 = (f32[4,64,256]{2,1,0:T(8,128)}, f32[4,64,256]{2,1,0:T(8,128)S(1)}, u32[]{:S(2)}) copy-start(f32[4,64,256]{2,1,0:T(8,128)S(1)} %maximum_select_fusion.8) | copy-start | bytes 786436
  62.4 7.1 %collective-permute-start.9 = (f32[2,64,128]{2,1,0:T(8,128)S(1)}, f32[2,64,128]{2,1,0:T(8,128)S(1)}, u32[]{:S(2)}, u32[]{:S(2)}) collective-permute-start(f32[2,64,128]{2,1,0:T(8,128)S(1)} %maximum_select_fusion.11), channel_id=1, source_target_pairs={{0,2},{1,3},{2,0},{3,1},{4,6},{5,7},{6,4},{7,5},{8,10},{9,11},{10,... | collective-permute-start | bytes 196616 | tf_op jit(solution)/shard_map/ppermute | solution.py:16
  64.2 16.2 %collective-permute-start.2 = (bf16[2048,128]{1,0:T(8,128)(2,1)}, bf16[2048,128]{1,0:T(8,128)(2,1)}, u32[]{:S(2)}, u32[]{:S(2)}) collective-permute-start(bf16[2048,128]{1,0:T(8,128)(2,1)} %collective-permute-done.1), channel_id=1, source_target_pairs={{0,1},{1,0},{2,3},{3,2},{4,5},{5,4},{6,7},{7,6},{8,9},{9,8},{10,11... | collective-permute-start | bytes 1572872 | tf_op jit(solution)/shard_map/ppermute | solution.py:16
  66.8 8.7 %collective-permute-start.16 = (f32[256,256]{1,0:T(8,128)S(1)}, f32[256,256]{1,0:T(8,128)}, u32[]{:S(2)}, u32[]{:S(2)}) collective-permute-start(f32[256,256]{1,0:T(8,128)S(1)} %fusion.79), channel_id=1, source_target_pairs={{0,4},{1,5},{2,6},{3,7},{4,0},{5,1},{6,2},{7,3},{8,12},{9,13},{10,... | collective-permute-start | bytes 786440 | tf_op jit(solution)/shard_map/ppermute | solution.py:16
  69.6 19.6 %collective-permute-start.7 = (f32[2,256,384]{1,2,0:T(8,128)S(1)}, f32[2,256,384]{1,2,0:T(8,128)}, u32[]{:S(2)}, u32[]{:S(2)}) collective-permute-start(f32[2,256,384]{1,2,0:T(8,128)S(1)} %maximum_select_fusion.4), channel_id=1, source_target_pairs={{0,2},{1,3},{2,0},{3,1},{4,6},{5,7},{6,4},{7,5},{8,10},{9,11},{10,... | collective-permute-start | bytes 2359304 | tf_op jit(solution)/shard_map/ppermute | solution.py:16
  70.3 0.7 copy-start.11
  75.4 10.4 %collective-permute-start.12 = (f32[256,384]{0,1:T(8,128)S(1)}, f32[256,384]{0,1:T(8,128)S(1)}, u32[]{:S(2)}, u32[]{:S(2)}) collective-permute-start(f32[256,384]{0,1:T(8,128)S(1)} %get-tuple-element.155), channel_id=1, source_target_pairs={{0,4},{1,5},{2,6},{3,7},{4,0},{5,1},{6,2},{7,3},{8,12},{9,13},{10,... | collective-permute-start | bytes 1179656 | tf_op jit(solution)/shard_map/ppermute | solution.py:16
  78.8 83.0 %collective-permute-start.3 = (bf16[2048,256]{1,0:T(8,128)(2,1)}, bf16[2048,256]{1,0:T(8,128)(2,1)}, u32[]{:S(2)}, u32[]{:S(2)}) collective-permute-start(bf16[2048,256]{1,0:T(8,128)(2,1)} %broadcast_select_fusion), channel_id=1, source_target_pairs={{0,1},{1,0},{2,3},{3,2},{4,5},{5,4},{6,7},{7,6},{8,9},{9,8},{10,11... | collective-permute-start | bytes 3145736 | tf_op jit(solution)/shard_map/ppermute | solution.py:16
  78.9 18.0 %collective-permute-start.17 = (f32[2,256,256]{2,1,0:T(8,128)}, f32[2,256,256]{2,1,0:T(8,128)}, u32[]{:S(2)}, u32[]{:S(2)}) collective-permute-start(f32[2,256,256]{2,1,0:T(8,128)} %maximum_select_fusion.7), channel_id=1, source_target_pairs={{0,8},{1,9},{2,10},{3,11},{4,12},{5,13},{6,14},{7,15},{8,0},{9,1},... | collective-permute-start | bytes 1572872 | tf_op jit(solution)/shard_map/ppermute | solution.py:16
  80.5 81.3 %collective-permute-start.5 = (bf16[2048,256]{1,0:T(8,128)(2,1)}, bf16[2048,256]{1,0:T(8,128)(2,1)}, u32[]{:S(2)}, u32[]{:S(2)}) collective-permute-start(bf16[2048,256]{1,0:T(8,128)(2,1)} %collective-permute-done.4), channel_id=1, source_target_pairs={{0,1},{1,0},{2,3},{3,2},{4,5},{5,4},{6,7},{7,6},{8,9},{9,8},{10,11... | collective-permute-start | bytes 3145736 | tf_op jit(solution)/shard_map/ppermute | solution.py:16
  85.9 63.1 %collective-permute-start.13 = (f32[2,256,384]{1,2,0:T(8,128)S(1)}, f32[2,256,384]{1,2,0:T(8,128)}, u32[]{:S(2)}, u32[]{:S(2)}) collective-permute-start(f32[2,256,384]{1,2,0:T(8,128)S(1)} %maximum_select_fusion.5), channel_id=1, source_target_pairs={{0,8},{1,9},{2,10},{3,11},{4,12},{5,13},{6,14},{7,15},{8,0},{9,1},... | collective-permute-start | bytes 2359304 | tf_op jit(solution)/shard_map/ppermute | solution.py:16
  91.9 2.1 %copy-start.10 = (f32[256,128]{1,0:T(8,128)S(1)}, f32[256,128]{1,0:T(8,128)}, u32[]{:S(2)}) copy-start(f32[256,128]{1,0:T(8,128)} %param.23) | copy-start | bytes 393220
  93.8 4.8 %copy-start.13 = (f32[16,128]{1,0:T(8,128)S(1)}, f32[16,128]{1,0:T(8,128)}, u32[]{:S(2)}) copy-start(f32[16,128]{1,0:T(8,128)} %param.25) | copy-start | bytes 24580
  94.0 52.6 %copy-start.17 = (pred[512]{0:T(512)(128)(4,1)S(1)}, pred[512]{0:T(512)(128)(4,1)}, u32[]{:S(2)}) copy-start(pred[512]{0:T(512)(128)(4,1)} %fusion.69) | copy-start | bytes 1540
  98.6 49.4 %copy-start.5 = (f32[4,64,256]{2,1,0:T(8,128)S(1)}, f32[4,64,256]{2,1,0:T(8,128)}, u32[]{:S(2)}) copy-start(f32[4,64,256]{2,1,0:T(8,128)} %copy-done.4) | copy-start | bytes 786436
  151.7 4.5 %copy-start.12 = (f32[4,64,128]{2,1,0:T(8,128)S(1)}, f32[4,64,128]{2,1,0:T(8,128)}, u32[]{:S(2)}) copy-start(f32[4,64,128]{2,1,0:T(8,128)} %copy-done.11) | copy-start | bytes 393220
  151.8 4.5 %copy-start.15 = (f32[256]{0:T(256)S(1)}, f32[256]{0:T(256)}, u32[]{:S(2)}) copy-start(f32[256]{0:T(256)} %sub.149) | copy-start | bytes 3076
  151.8 4.5 %copy-start.16 = (pred[1024]{0:T(1024)(128)(4,1)S(1)}, pred[1024]{0:T(1024)(128)(4,1)}, u32[]{:S(2)}) copy-start(pred[1024]{0:T(1024)(128)(4,1)} %fusion.66) | copy-start | bytes 3076
  151.8 6.8 %copy-start.8 = (f32[256,256]{1,0:T(8,128)S(1)}, f32[256,256]{1,0:T(8,128)}, u32[]{:S(2)}) copy-start(f32[256,256]{1,0:T(8,128)} %fusion.80) | copy-start | bytes 786436
  154.8 3.7 %copy-start.3 = (f32[4,256,384]{2,1,0:T(8,128)S(1)}, f32[4,256,384]{2,1,0:T(8,128)}, u32[]{:S(2)}) copy-start(f32[4,256,384]{2,1,0:T(8,128)} %copy.35) | copy-start | bytes 4718596
  156.2 3.3 %copy-start.7 = (f32[256,256]{1,0:T(8,128)S(1)}, f32[256,256]{1,0:T(8,128)}, u32[]{:S(2)}) copy-start(f32[256,256]{1,0:T(8,128)} %param.21) | copy-start | bytes 786436
  158.5 1.5 copy-start.9
  181.1 1.3 copy-start.2
where the time goes:
time: 209 us; the launch traced here: 208 us
  matrix products  49.2 us (24%)
  other arithmetic  49 us (23%)
  blocking collectives  47.8 us (23%)
  local copies, waits for them, and re-layouts  21.9 us (10%)
  waiting for transfers between devices  20.1 us (10%)
  starting transfers between devices  14.8 us (7%)
  between operations  4.34 us (2%)
    all_gather x1, blocking collectives, per_device(): top_all = lax.all_gather(top_piece, 'leaf', axis=0, tiled=True)  47.8 us
    dot_general x12, matrix products, one_block(): jnp.dot(tile.astype(jnp.bfloat16), values, preferred_element_type=jnp.flo...  33.6 us
    ppermute x18, waiting for transfers between devices, from_partner(): lax.ppermute(shard, axis, [(i, i ^ 1 << stride) for i in range(lax.axis_s...  20.1 us
    ppermute x18, starting transfers between devices, from_partner(): lax.ppermute(shard, axis, [(i, i ^ 1 << stride) for i in range(lax.axis_s...  14.8 us
    reduce_sum x12, other arithmetic, one_block(): row_norm = jnp.sum(jnp.square(row_points.astype(jnp.float32)), axis=1)  12.6 us
    gather x1, local copies, waits for them, and re-layouts, per_device(): rhs = jnp.take(charges, order[0], axis=0)  8 us
    select_n x6, other arithmetic, group_collect(): jnp.where(low_value == 0, jnp.stack([mine, other]), jnp.stack([other, min...  6.97 us
    dot_general x3, matrix products, couple(): products = jnp.dot(left, right.T, precision=highest)  5.77 us
  transfers between devices with their start and end apart: 18, of which 4 were waited for; matrix products, arithmetic and copies ran while one was open for 31% of the time, Pallas kernels for 0%

commit v1 on v0

v1 whole, which is shorter than its diff:
```python
import functools

import jax
import jax.numpy as jnp
from jax import lax
from jax.experimental import pallas as pl
from jax.experimental.pallas import tpu as pltpu
from jax.sharding import PartitionSpec as P

MESH = pl.DeviceIdType.MESH
F32, BF16 = jnp.float32, jnp.bfloat16
CHUNKS = 8
EARLY = 5
ROWS = 512


def mm(a, b, ca=1, cb=0):
    return lax.dot_general(a, b, (((ca,), (cb,)), ((), ())), preferred_element_type=F32)


def split3(x):
    high = x.astype(BF16).astype(F32)
    middle = (x - high).astype(BF16).astype(F32)
    return high, middle, x - high - middle


def norm_column(p):
    wide = p.astype(F32)
    return jnp.sum(wide * wide, axis=1, keepdims=True)


def norm_lanes(p, one_scale, norm_scale, norm_first):
    high, middle, low = split3(norm_column(p))
    lane = lax.broadcasted_iota(jnp.int32, (p.shape[0], 128), 1)
    first = 0 if norm_first else 3
    ones = jnp.where(lane < 6, one_scale, 0.0)
    out = jnp.where(lane == first, high * norm_scale, ones)
    out = jnp.where(lane == first + 1, middle * norm_scale, out)
    out = jnp.where(lane == first + 2, low * norm_scale, out)
    return out.astype(BF16)


def couple(left, right):
    scale = 2.0 / left.shape[1]
    wide = right.astype(F32)
    square = wide * wide
    high = square.astype(BF16)
    low = (square - high.astype(F32)).astype(BF16)
    ones = jnp.ones((8, left.shape[1]), BF16)
    right_norm = (mm(ones, high, 1, 1) + mm(ones, low, 1, 1))[0:1, :]
    return jnp.exp((2.0 * mm(left, right, 1, 1) - norm_column(left) - right_norm) * scale).astype(BF16)


def kernel(n, near, points, charges, order, bases, lift, nlift, zleaf, znode, ztop, out,
           rhs, laug, raug, acc, p1, p2, p3, r1, r2, r3, cp, cr,
           c0, c0x, z0, z0x, ut, rs, nl, z1, z1s, z2, nv, nvs, c2, c2o, z2o, f1,
           ssem, rsem):
    me = lax.axis_index("leaf")
    leaf, dim = points.shape
    rank = lift.shape[0]
    quarter = rank // 4
    sixteenth = rank // 16
    nodes = n // 16
    slot = me % 4
    group = me // 4 % 4
    part = me % 16
    node = me // 16
    step = leaf // CHUNKS

    def flip(bits):
        if bits == 1:
            return me + 1 - 2 * (me % 2)
        if bits == 2:
            return me + 2 - 4 * (me // 2 % 2)
        if bits == 3:
            return me - slot + 3 - slot
        if bits == 4:
            return me + 4 - 8 * (me // 4 % 2)
        if bits == 8:
            return me + 8 - 16 * (me // 8 % 2)
        return me - 4 * group + 4 * (3 - group)

    def flip_slot(bits):
        if bits == 1:
            return slot + 1 - 2 * (slot % 2)
        if bits == 2:
            return slot + 2 - 4 * (slot // 2)
        return 3 - slot

    others = [(node + d) % nodes * 16 + part for d in range(1, nodes)]

    barrier = pltpu.get_barrier_semaphore()
    partners = [flip(b) for b in (1, 2, 3, 4, 8, 12)] + others
    for other in partners:
        pl.semaphore_signal(barrier, inc=1, device_id=(other,), device_id_type=MESH)

    count = [0]
    started = []

    def send(src, dst, device):
        i = count[0]
        count[0] += 1
        copy = pltpu.make_async_remote_copy(
            src_ref=src, dst_ref=dst, send_sem=ssem.at[i], recv_sem=rsem.at[i],
            device_id=(device,), device_id_type=MESH)
        copy.start()
        started.append(copy)
        return copy

    mine = pl.ds(pl.multiple_of(slot * quarter, quarter), quarter)
    mine16 = pl.ds(pl.multiple_of(part * sixteenth, sixteenth), sixteenth)
    mine64 = pl.ds(pl.multiple_of(group * quarter, quarter), quarter)
    z1[mine, :] = znode[...].astype(BF16)
    nl[mine, :] = nlift[...].astype(BF16)
    z2[mine16, :] = ztop[...].astype(BF16)
    z0[...] = zleaf[...].astype(BF16)
    pl.semaphore_wait(barrier, len(partners))

    points_one = send(points, p1, flip(1))
    points_two = send(points, p2, flip(2))
    phase_a = []
    for b in (1, 2, 3):
        phase_a.append(send(z1.at[mine, :], z1.at[mine, :], flip(b)))
        phase_a.append(send(nl.at[mine, :], nl.at[mine, :], flip(b)))
        phase_a.append(send(z2.at[mine16, :], z2.at[mine16, :], flip(b)))

    def permute(block, carry):
        rows = pl.ds(pl.multiple_of(block * 128, 128), 128)
        index = jnp.broadcast_to(order[0:1, rows].astype(F32), (128, 128)).T
        lane = lax.broadcasted_iota(jnp.int32, (128, 128), 1).astype(F32)
        chosen = jnp.concatenate(
            [jnp.where(index == lane + 128.0 * j, 1.0, 0.0).astype(BF16) for j in range(leaf // 128)], 1)
        rhs[rows, :] = mm(chosen, charges[...]).astype(BF16)
        return carry

    lax.fori_loop(0, leaf // 128, permute, 0)

    own = mm(rhs[...], bases[...], 0, 0).astype(BF16)
    c0[...] = own
    lift16 = lift[...].astype(BF16)
    up = mm(own, lift16)
    ut[...] = up.astype(BF16)
    phase_up = []
    for b in (1, 2, 3):
        there = pl.ds(pl.multiple_of(flip_slot(b) * quarter, quarter), quarter)
        phase_up.append(send(ut.at[there, :], rs.at[b - 1], flip(b)))
    rhs_one = send(rhs, r1, flip(1))
    rhs_two = []

    def send_chunk(c):
        rows = pl.ds(c * step, step)
        rhs_two.append(send(rhs.at[rows, :], r2.at[rows, :], flip(2)))

    phase_far = []
    send_chunk(0)
    for b in (1, 2):
        phase_far.append(send(c0, c0x.at[b - 1], flip(b)))
        phase_far.append(send(z0, z0x.at[b - 1], flip(b)))
    for c in range(1, EARLY):
        send_chunk(c)

    def augment(block, carry):
        rows = pl.ds(pl.multiple_of(block * ROWS, ROWS), ROWS)
        p = points[rows, :]
        laug[rows, 0:dim] = (p.astype(F32) * (4.0 / dim)).astype(BF16)
        laug[rows, dim:] = norm_lanes(p, -2.0 / dim, -2.0 / dim, False)
        raug[rows, 0:dim] = p
        raug[rows, dim:] = norm_lanes(p, 1.0, 1.0, True)
        return carry

    lax.fori_loop(0, leaf // ROWS, augment, 0)

    def tiles(rows, right, width):
        left = laug[rows, :]
        return jnp.concatenate(
            [jnp.exp(mm(left, right[j:j + 512, :], 1, 1)).astype(BF16) for j in range(0, width, 512)], 1)

    def own_tile(block, carry):
        rows = pl.ds(pl.multiple_of(block * ROWS, ROWS), ROWS)
        acc[rows, :] = mm(tiles(rows, raug, leaf), rhs[...])
        return carry

    blocks = leaf // ROWS
    lax.fori_loop(0, blocks // 2, own_tile, 0)

    for copy in phase_a:
        copy.wait_recv()
    phase_b = []
    for i, b in enumerate((4, 8, 12)):
        phase_b.append(send(z1, z1s.at[i], flip(b)))
        phase_b.append(send(z2.at[mine64, :], z2.at[mine64, :], flip(b)))
    for copy in phase_up:
        copy.wait_recv()
    total = ut[mine, :].astype(F32)
    for i in range(3):
        total = total + rs[i].astype(F32)
    nv[0] = total.astype(BF16)
    lifted = mm(total.astype(BF16), nl[...])
    nv[1] = lifted.astype(BF16)
    phase_two = [send(nv, nvs.at[i], flip(b)) for i, b in enumerate((4, 8, 12))]

    lax.fori_loop(blocks // 2, blocks, own_tile, 0)

    points_two.wait_recv()
    points_three = send(p2, p3, flip(1))
    for copy in phase_b:
        copy.wait_recv()
    for copy in phase_two:
        copy.wait_recv()
    for i in range(3):
        lifted = lifted + nvs[i, 1].astype(F32)
    c2[...] = lifted.astype(BF16)
    phase_top = []
    for d, other in enumerate(others):
        phase_top.append(send(c2, c2o.at[d], other))
        phase_top.append(send(z2, z2o.at[d], other))

    side = mm(nvs[0, 0], couple(z1s[0], z1[...]))
    for i in (1, 2):
        side = side + mm(nvs[i, 0], couple(z1s[i], z1[...]))

    first = near[0, 0] - me
    second = near[0, 1] - me
    one = 1 - 2 * (me % 2)
    near_one = jnp.logical_or(first == one, second == one)

    def choose(a, b):
        return jnp.where(near_one, a.astype(F32), b.astype(F32)).astype(BF16)

    phase_rhs = []

    def relay(c):
        rhs_two[c].wait_recv()
        rows = pl.ds(c * step, step)
        phase_rhs.append(send(r2.at[rows, :], r3.at[rows, :], flip(1)))

    def near_chunk(c, final):
        rows = pl.ds(c * step, step)
        phase_rhs[c].wait_recv()
        picked = choose(p1[rows, :], p2[rows, :])
        cp[0:step, 0:dim] = picked
        cp[0:step, dim:] = norm_lanes(picked, 1.0, 1.0, True)
        diagonal = p3[rows, :]
        cp[step:, 0:dim] = diagonal
        cp[step:, dim:] = norm_lanes(diagonal, 1.0, 1.0, True)
        cr[0:step, :] = choose(r1[rows, :], r2[rows, :])
        cr[step:, :] = r3[rows, :]

        def body(block, carry):
            rows = pl.ds(pl.multiple_of(block * ROWS, ROWS), ROWS)
            value = acc[rows, :] + mm(tiles(rows, cp, 2 * step), cr[...])
            if final:
                out[rows, :] = value.astype(BF16)
            else:
                acc[rows, :] = value
            return carry

        lax.fori_loop(0, blocks, body, 0)

    relay(0)
    rhs_one.wait_recv()
    points_one.wait_recv()
    for copy in phase_top:
        copy.wait_recv()
    field = mm(c2o[0], couple(z2o[0], z2[...]))
    for d in range(1, nodes - 1):
        field = field + mm(c2o[d], couple(z2o[d], z2[...]))
    field1 = side + mm(field.astype(BF16), nl[...], 1, 1)
    f1[mine, :] = field1.astype(BF16)
    phase_down = [send(f1.at[mine, :], f1.at[mine, :], flip(b)) for b in (1, 2, 3)]
    for c in range(EARLY, CHUNKS):
        send_chunk(c)
    points_three.wait_recv()
    for c in range(1, CHUNKS):
        relay(c)
        near_chunk(c - 1, False)
        if c == 5:
            for copy in phase_far:
                copy.wait_recv()
            for copy in phase_down:
                copy.wait_recv()
            far_z = choose(z0x[1], z0x[0])
            far_c = choose(c0x[1], c0x[0])
            field0 = mm(far_c, couple(far_z, z0[...])) + mm(f1[...], lift[...].astype(BF16), 1, 1)
            c0x[0] = field0.astype(BF16)

            def descend(block, carry):
                rows = pl.ds(pl.multiple_of(block * ROWS, ROWS), ROWS)
                acc[rows, :] += mm(bases[rows, :], c0x[0], 1, 1)
                return carry

            lax.fori_loop(0, blocks, descend, 0)
    near_chunk(CHUNKS - 1, True)
    for copy in started:
        copy.wait_send()


def per_device(n, near, points, charges, order, bases, lift, nlift, zleaf, znode, ztop):
    leaf, dim = points.shape
    nrhs = charges.shape[1]
    rank = lift.shape[0]
    quarter = rank // 4
    nodes = n // 16
    copies = 11 + 3 + 1 + CHUNKS + 4 + 6 + 3 + 1 + 2 * (nodes - 1) + CHUNKS + 3
    v = pltpu.VMEM
    vmem = pl.BlockSpec(memory_space=pltpu.VMEM)
    return pl.pallas_call(
        functools.partial(kernel, n),
        out_shape=jax.ShapeDtypeStruct((leaf, nrhs), BF16),
        in_specs=[pl.BlockSpec(memory_space=pltpu.SMEM)] + [vmem] * 9,
        out_specs=vmem,
        scratch_shapes=[
            v((leaf, nrhs), BF16), v((leaf, 2 * dim), BF16), v((leaf, 2 * dim), BF16),
            v((leaf, nrhs), F32),
            v((leaf, dim), BF16), v((leaf, dim), BF16), v((leaf, dim), BF16),
            v((leaf, nrhs), BF16), v((leaf, nrhs), BF16), v((leaf, nrhs), BF16),
            v((2 * leaf // CHUNKS, 2 * dim), BF16), v((2 * leaf // CHUNKS, nrhs), BF16),
            v((nrhs, rank), BF16), v((2, nrhs, rank), BF16),
            v((rank, dim), BF16), v((2, rank, dim), BF16),
            v((nrhs, rank), BF16), v((3, quarter, rank), BF16),
            v((rank, rank), BF16), v((rank, dim), BF16), v((3, rank, dim), BF16),
            v((rank, dim), BF16),
            v((2, quarter, rank), BF16), v((3, 2, quarter, rank), BF16),
            v((quarter, rank), BF16), v((nodes - 1, quarter, rank), BF16),
            v((nodes - 1, rank, dim), BF16), v((nrhs, rank), BF16),
            pltpu.SemaphoreType.DMA((copies,)), pltpu.SemaphoreType.DMA((copies,)),
        ],
        compiler_params=pltpu.CompilerParams(
            collective_id=0, has_side_effects=True, vmem_limit_bytes=60 * 1024 * 1024),
    )(near, points, charges, order, bases, lift, nlift, zleaf, znode, ztop)


def solution(mesh):
    n = mesh.shape["leaf"]

    def body(points, charges, order, near, bases, lift, nlift, zleaf, znode, ztop):
        return per_device(n, near, points, charges, order, bases, lift, nlift, zleaf, znode, ztop)

    return jax.shard_map(
        body, mesh=mesh, in_specs=(P("leaf", None),) * 10, out_specs=P("leaf", None), check_vma=False)
```

time: 209 us -> 64.3 us (0.31)
  Pallas kernels: 0 us -> 61.8 us
  matrix products: 49.2 us -> 0 us
  other arithmetic: 49 us -> 0 us
  blocking collectives: 47.8 us -> 0 us
  waiting for transfers between devices: 20.1 us -> 0 us
  local copies, waits for them, and re-layouts: 21.9 us -> 2.26 us
  starting transfers between devices: 14.8 us -> 0 us
  between operations: 4.34 us -> 0.01 us
    pallas_call x0 -> x1, Pallas kernels: none -> 61.8 us  [per_device(): pl.pallas_call(functools.partial(kernel, n), out_shape=jax.ShapeDtypeStru...]
    dot_general x24 -> x0, matrix products: 49.2 us -> none  [the longest x12 33.6 us: one_block(): jnp.dot(tile.astype(jnp.bfloat16), values, preferred_element_type=jnp.flo...]
    all_gather x1 -> x0, blocking collectives: 47.8 us -> none  [per_device(): top_all = lax.all_gather(top_piece, 'leaf', axis=0, tiled=True)]
    reduce_sum x22 -> x0, other arithmetic: 23.9 us -> none  [the longest x12 12.6 us: one_block(): row_norm = jnp.sum(jnp.square(row_points.astype(jnp.float32)), axis=1)]
    ppermute x18 -> x0, waiting for transfers between devices: 20.1 us -> none  [from_partner(): lax.ppermute(shard, axis, [(i, i ^ 1 << stride) for i in range(lax.axis_s...]
    select_n x12 -> x0, other arithmetic: 17.7 us -> none  [the longest x6 6.97 us: group_collect(): jnp.where(low_value == 0, jnp.stack([mine, other]), jnp.stack([other, min...]
    ppermute x18 -> x0, starting transfers between devices: 14.8 us -> none  [from_partner(): lax.ppermute(shard, axis, [(i, i ^ 1 << stride) for i in range(lax.axis_s...]
    gather x1 -> x0, local copies, waits for them, and re-layouts: 8 us -> none  [per_device(): rhs = jnp.take(charges, order[0], axis=0)]
  transfers between devices with their start and end apart: 18 -> 0, of which waited for: 4 -> 0; matrix products, arithmetic and copies ran while one was open for 31% -> 0% of each run, Pallas kernels for 0% -> 0%
where the time goes in v1:
time: 64.3 us; the launch traced here: 64.1 us
  Pallas kernels  61.8 us (96%)
  local copies, waits for them, and re-layouts  2.26 us (4%)
    pallas_call x1, Pallas kernels, per_device(): pl.pallas_call(functools.partial(kernel, n), out_shape=jax.ShapeDtypeStru...  61.8 us
    unnamed x1, local copies, waits for them, and re-layouts  2.26 us

profile of v1, /device:TPU:0, one launch (start us, length us, event | category | flops | bytes accessed | tf_op | source)
XLA Modules:
  0.0 64.1 jit_solution(473160114830001445)
XLA Ops:
  0.0 61.8 %shard_map.100 = bf16[2048,256]{1,0:T(8,128)(2,1)} custom-call(s32[1,2]{1,0:T(1,128)} %near.1, bf16[2048,128]{1,0:T(8,128)(2,1)} %points.1, bf16[2048,256]{1,0:T(8,128)(2,1)} %charges.1, s32[1,2048]{1,0:T(1,128)} %order.1, bf16[2048,256]{1,0:T(8,128)(2,1)} %bases.1, f32[256,256]{1,0:T(8,128)} %lift.1, f32[64,256]{1,0:T(8,128)} %nlift.1, f32[256,128]{1,0:T(8,128)} %zleaf.1, ...), custom_call_target="tpu_custom_call" | custom-call | tf_op jit(solution)/shard_map/pallas_call | solution.py:307
  61.8 2.3 %copy.12 = bf16[2048,256]{1,0:T(8,128)(2,1)} copy(bf16[2048,256]{1,0:T(8,128)(2,1)} %shard_map.100) | data formatting | bytes 2097152

commit v2 on v1

--- a/solution.py
+++ b/solution.py
@@ -10,7 +10,7 @@
 MESH = pl.DeviceIdType.MESH
 F32, BF16 = jnp.float32, jnp.bfloat16
 CHUNKS = 8
-EARLY = 5
+EARLY = 6
 ROWS = 512
 
 
@@ -51,14 +51,15 @@
     return jnp.exp((2.0 * mm(left, right, 1, 1) - norm_column(left) - right_norm) * scale).astype(BF16)
 
 
-def kernel(n, near, points, charges, order, bases, lift, nlift, zleaf, znode, ztop, out,
-           rhs, laug, raug, acc, p1, p2, p3, r1, r2, r3, cp, cr,
-           c0, c0x, z0, z0x, ut, rs, nl, z1, z1s, z2, nv, nvs, c2, c2o, z2o, f1,
-           ssem, rsem):
+def kernel(n, near, points_in, charges_in, bases_in, order, lift, nlift, zleaf, znode, ztop, out,
+           points, charges, bases, rhs, laug, raug, acc, p1, p2, p3, r1, r2, r3, cp, cr,
+           c0, c0x, z0, z0x, ut, us, rs, nl, z1, z1s, z2, nv, nvs, c2, c2o, z2o, f1,
+           ssem, rsem, lsem):
     me = lax.axis_index("leaf")
     leaf, dim = points.shape
     rank = lift.shape[0]
     quarter = rank // 4
+    head = leaf * 3 // 4
     sixteenth = rank // 16
     nodes = n // 16
     slot = me % 4
@@ -94,6 +95,10 @@
     for other in partners:
         pl.semaphore_signal(barrier, inc=1, device_id=(other,), device_id_type=MESH)
 
+    loads = [pltpu.make_async_copy(a, b, lsem.at[i]) for i, (a, b) in enumerate(
+        ((charges_in, charges), (bases_in, bases), (points_in, points)))]
+    for copy in loads:
+        copy.start()
     count = [0]
     started = []
 
@@ -116,13 +121,21 @@
     z0[...] = zleaf[...].astype(BF16)
     pl.semaphore_wait(barrier, len(partners))
 
-    points_one = send(points, p1, flip(1))
-    points_two = send(points, p2, flip(2))
-    phase_a = []
-    for b in (1, 2, 3):
-        phase_a.append(send(z1.at[mine, :], z1.at[mine, :], flip(b)))
-        phase_a.append(send(nl.at[mine, :], nl.at[mine, :], flip(b)))
-        phase_a.append(send(z2.at[mine16, :], z2.at[mine16, :], flip(b)))
+    def at_slot(bits):
+        where = flip_slot(bits) if bits else slot
+        return pl.ds(pl.multiple_of(where * quarter, quarter), quarter)
+
+    far16 = pl.ds(pl.multiple_of(flip(2) % 16 * sixteenth, sixteenth), sixteenth)
+    phase_a2 = [send(z1.at[mine, :], z1.at[mine, :], flip(2)),
+                send(nl.at[mine, :], nl.at[mine, :], flip(2)),
+                send(z2.at[mine16, :], z2.at[mine16, :], flip(2))]
+    top, rest = pl.ds(0, head), pl.ds(head, leaf - head)
+    points_two = send(points_in.at[top, :], p2.at[top, :], flip(2))
+    phase_a = [send(z1.at[mine, :], z1.at[mine, :], flip(1)),
+               send(nl.at[mine, :], nl.at[mine, :], flip(1)),
+               send(z2.at[mine16, :], z2.at[mine16, :], flip(1))]
+    points_one = send(points_in, p1, flip(1))
+    loads[0].wait()
 
     def permute(block, carry):
         rows = pl.ds(pl.multiple_of(block * 128, 128), 128)
@@ -135,28 +148,37 @@
 
     lax.fori_loop(0, leaf // 128, permute, 0)
 
+    loads[1].wait()
     own = mm(rhs[...], bases[...], 0, 0).astype(BF16)
     c0[...] = own
-    lift16 = lift[...].astype(BF16)
-    up = mm(own, lift16)
+    up = mm(own, lift[...].astype(BF16))
     ut[...] = up.astype(BF16)
-    phase_up = []
-    for b in (1, 2, 3):
-        there = pl.ds(pl.multiple_of(flip_slot(b) * quarter, quarter), quarter)
-        phase_up.append(send(ut.at[there, :], rs.at[b - 1], flip(b)))
+    up_near = send(ut.at[at_slot(1), :], rs.at[0], flip(1))
+    up_cross = send(ut.at[at_slot(3), :], rs.at[1], flip(1))
     rhs_one = send(rhs, r1, flip(1))
+    for copy in phase_a2:
+        copy.wait_recv()
+    phase_a.append(send(z1.at[at_slot(2), :], z1.at[at_slot(2), :], flip(1)))
+    phase_a.append(send(nl.at[at_slot(2), :], nl.at[at_slot(2), :], flip(1)))
+    phase_a.append(send(z2.at[far16, :], z2.at[far16, :], flip(1)))
     rhs_two = []
 
     def send_chunk(c):
         rows = pl.ds(c * step, step)
         rhs_two.append(send(rhs.at[rows, :], r2.at[rows, :], flip(2)))
 
+    loads[2].wait()
+    up_cross.wait_recv()
+    us[...] = (ut[at_slot(2), :].astype(F32) + rs[1].astype(F32)).astype(BF16)
+    up_two = send(us, rs.at[2], flip(2))
+    points_rest = send(points_in.at[rest, :], p2.at[rest, :], flip(2))
+    send_chunk(0)
+    send_chunk(1)
     phase_far = []
-    send_chunk(0)
     for b in (1, 2):
         phase_far.append(send(c0, c0x.at[b - 1], flip(b)))
         phase_far.append(send(z0, z0x.at[b - 1], flip(b)))
-    for c in range(1, EARLY):
+    for c in range(2, EARLY):
         send_chunk(c)
 
     def augment(block, carry):
@@ -181,28 +203,27 @@
         return carry
 
     blocks = leaf // ROWS
-    lax.fori_loop(0, blocks // 2, own_tile, 0)
-
     for copy in phase_a:
         copy.wait_recv()
     phase_b = []
     for i, b in enumerate((4, 8, 12)):
         phase_b.append(send(z1, z1s.at[i], flip(b)))
         phase_b.append(send(z2.at[mine64, :], z2.at[mine64, :], flip(b)))
-    for copy in phase_up:
-        copy.wait_recv()
-    total = ut[mine, :].astype(F32)
-    for i in range(3):
-        total = total + rs[i].astype(F32)
+
+    lax.fori_loop(0, blocks // 2, own_tile, 0, unroll=2)
+
+    up_near.wait_recv()
+    up_two.wait_recv()
+    total = ut[mine, :].astype(F32) + rs[0].astype(F32) + rs[2].astype(F32)
     nv[0] = total.astype(BF16)
     lifted = mm(total.astype(BF16), nl[...])
     nv[1] = lifted.astype(BF16)
     phase_two = [send(nv, nvs.at[i], flip(b)) for i, b in enumerate((4, 8, 12))]
-
-    lax.fori_loop(blocks // 2, blocks, own_tile, 0)
-
     points_two.wait_recv()
-    points_three = send(p2, p3, flip(1))
+    points_three = [send(p2.at[top, :], p3.at[top, :], flip(1))]
+
+    lax.fori_loop(blocks // 2, blocks, own_tile, 0, unroll=2)
+
     for copy in phase_b:
         copy.wait_recv()
     for copy in phase_two:
@@ -214,6 +235,8 @@
     for d, other in enumerate(others):
         phase_top.append(send(c2, c2o.at[d], other))
         phase_top.append(send(z2, z2o.at[d], other))
+    points_rest.wait_recv()
+    points_three.append(send(p2.at[rest, :], p3.at[rest, :], flip(1)))
 
     side = mm(nvs[0, 0], couple(z1s[0], z1[...]))
     for i in (1, 2):
@@ -255,11 +278,15 @@
                 acc[rows, :] = value
             return carry
 
-        lax.fori_loop(0, blocks, body, 0)
+        lax.fori_loop(0, blocks, body, 0, unroll=2)
 
     relay(0)
     rhs_one.wait_recv()
     points_one.wait_recv()
+    for copy in points_three:
+        copy.wait_recv()
+    relay(1)
+    near_chunk(0, False)
     for copy in phase_top:
         copy.wait_recv()
     field = mm(c2o[0], couple(z2o[0], z2[...]))
@@ -267,14 +294,17 @@
         field = field + mm(c2o[d], couple(z2o[d], z2[...]))
     field1 = side + mm(field.astype(BF16), nl[...], 1, 1)
     f1[mine, :] = field1.astype(BF16)
-    phase_down = [send(f1.at[mine, :], f1.at[mine, :], flip(b)) for b in (1, 2, 3)]
+    down_two = send(f1.at[mine, :], f1.at[mine, :], flip(2))
+    phase_down = [send(f1.at[mine, :], f1.at[mine, :], flip(1))]
     for c in range(EARLY, CHUNKS):
         send_chunk(c)
-    points_three.wait_recv()
-    for c in range(1, CHUNKS):
+    for c in range(2, CHUNKS):
         relay(c)
         near_chunk(c - 1, False)
-        if c == 5:
+        if c == CHUNKS - 2:
+            down_two.wait_recv()
+            phase_down.append(send(f1.at[at_slot(2), :], f1.at[at_slot(2), :], flip(1)))
+        if c == CHUNKS - 1:
             for copy in phase_far:
                 copy.wait_recv()
             for copy in phase_down:
@@ -301,15 +331,16 @@
     rank = lift.shape[0]
     quarter = rank // 4
     nodes = n // 16
-    copies = 11 + 3 + 1 + CHUNKS + 4 + 6 + 3 + 1 + 2 * (nodes - 1) + CHUNKS + 3
+    copies = 8 + 2 + 1 + 3 + 2 + CHUNKS + 4 + 6 + 3 + 2 + 2 * (nodes - 1) + CHUNKS + 3
     v = pltpu.VMEM
     vmem = pl.BlockSpec(memory_space=pltpu.VMEM)
     return pl.pallas_call(
         functools.partial(kernel, n),
         out_shape=jax.ShapeDtypeStruct((leaf, nrhs), BF16),
-        in_specs=[pl.BlockSpec(memory_space=pltpu.SMEM)] + [vmem] * 9,
+        in_specs=[pl.BlockSpec(memory_space=pltpu.SMEM)] + [pl.BlockSpec(memory_space=pl.ANY)] * 3 + [vmem] * 6,
         out_specs=vmem,
         scratch_shapes=[
+            v((leaf, dim), BF16), v((leaf, nrhs), BF16), v((leaf, rank), BF16),
             v((leaf, nrhs), BF16), v((leaf, 2 * dim), BF16), v((leaf, 2 * dim), BF16),
             v((leaf, nrhs), F32),
             v((leaf, dim), BF16), v((leaf, dim), BF16), v((leaf, dim), BF16),
@@ -317,17 +348,18 @@
             v((2 * leaf // CHUNKS, 2 * dim), BF16), v((2 * leaf // CHUNKS, nrhs), BF16),
             v((nrhs, rank), BF16), v((2, nrhs, rank), BF16),
             v((rank, dim), BF16), v((2, rank, dim), BF16),
-            v((nrhs, rank), BF16), v((3, quarter, rank), BF16),
+            v((nrhs, rank), BF16), v((quarter, rank), BF16), v((3, quarter, rank), BF16),
             v((rank, rank), BF16), v((rank, dim), BF16), v((3, rank, dim), BF16),
             v((rank, dim), BF16),
             v((2, quarter, rank), BF16), v((3, 2, quarter, rank), BF16),
             v((quarter, rank), BF16), v((nodes - 1, quarter, rank), BF16),
             v((nodes - 1, rank, dim), BF16), v((nrhs, rank), BF16),
             pltpu.SemaphoreType.DMA((copies,)), pltpu.SemaphoreType.DMA((copies,)),
+            pltpu.SemaphoreType.DMA((3,)),
         ],
         compiler_params=pltpu.CompilerParams(
             collective_id=0, has_side_effects=True, vmem_limit_bytes=60 * 1024 * 1024),
-    )(near, points, charges, order, bases, lift, nlift, zleaf, znode, ztop)
+    )(near, points, charges, bases, order, lift, nlift, zleaf, znode, ztop)
 
 
 def solution(mesh):

time: 64.3 us -> 57.3 us (0.89)
  Pallas kernels: 61.8 us -> 54.9 us
    pallas_call x1, Pallas kernels: 61.8 us -> 54.9 us  [per_device(): pl.pallas_call(functools.partial(kernel, n), out_shape=jax.ShapeDtypeStru...]
where the time goes in v2:
time: 57.3 us; the launch traced here: 57.2 us
  Pallas kernels  54.9 us (96%)
  local copies, waits for them, and re-layouts  2.26 us (4%)
    pallas_call x1, Pallas kernels, per_device(): pl.pallas_call(functools.partial(kernel, n), out_shape=jax.ShapeDtypeStru...  54.9 us
    unnamed x1, local copies, waits for them, and re-layouts  2.26 us

profile of v2, /device:TPU:0, one launch (start us, length us, event | category | flops | bytes accessed | tf_op | source)
XLA Modules:
  0.0 57.2 jit_solution(15036086956454891152)
XLA Ops:
  0.0 54.9 %shard_map.100 = bf16[2048,256]{1,0:T(8,128)(2,1)} custom-call(s32[1,2]{1,0:T(1,128)} %near.1, bf16[2048,128]{1,0:T(8,128)(2,1)} %points_in.1, bf16[2048,256]{1,0:T(8,128)(2,1)} %charges_in.1, bf16[2048,256]{1,0:T(8,128)(2,1)} %bases_in.1, s32[1,2048]{1,0:T(1,128)} %order.1, f32[256,256]{1,0:T(8,128)} %lift.1, f32[64,256]{1,0:T(8,128)} %nlift.1, ...), custom_call_target="tpu_custom_call" | custom-call | tf_op jit(solution)/shard_map/pallas_call | solution.py:337
  54.9 2.3 %copy.12 = bf16[2048,256]{1,0:T(8,128)(2,1)} copy(bf16[2048,256]{1,0:T(8,128)(2,1)} %shard_map.100) | data formatting | bytes 2097152

commit v3 on v2

--- a/solution.py
+++ b/solution.py
@@ -11,7 +11,7 @@
 F32, BF16 = jnp.float32, jnp.bfloat16
 CHUNKS = 8
 EARLY = 6
-ROWS = 512
+ROWS = 1024
 
 
 def mm(a, b, ca=1, cb=0):
@@ -210,7 +210,7 @@
         phase_b.append(send(z1, z1s.at[i], flip(b)))
         phase_b.append(send(z2.at[mine64, :], z2.at[mine64, :], flip(b)))
 
-    lax.fori_loop(0, blocks // 2, own_tile, 0, unroll=2)
+    lax.fori_loop(0, blocks // 2, own_tile, 0)
 
     up_near.wait_recv()
     up_two.wait_recv()
@@ -222,7 +222,7 @@
     points_two.wait_recv()
     points_three = [send(p2.at[top, :], p3.at[top, :], flip(1))]
 
-    lax.fori_loop(blocks // 2, blocks, own_tile, 0, unroll=2)
+    lax.fori_loop(blocks // 2, blocks, own_tile, 0)
 
     for copy in phase_b:
         copy.wait_recv()

time: 57.3 us -> 56.1 us (0.979)
  Pallas kernels: 54.9 us -> 53.7 us
    pallas_call x1, Pallas kernels: 54.9 us -> 53.7 us  [per_device(): pl.pallas_call(functools.partial(kernel, n), out_shape=jax.ShapeDtypeStru...]
where the time goes in v3:
time: 56.1 us; the launch traced here: 56 us
  Pallas kernels  53.7 us (96%)
  local copies, waits for them, and re-layouts  2.26 us (4%)
    pallas_call x1, Pallas kernels, per_device(): pl.pallas_call(functools.partial(kernel, n), out_shape=jax.ShapeDtypeStru...  53.7 us
    unnamed x1, local copies, waits for them, and re-layouts  2.26 us

profile of v3, /device:TPU:0, one launch (start us, length us, event | category | flops | bytes accessed | tf_op | source)
XLA Modules:
  0.0 56.0 jit_solution(12562611784121899455)
XLA Ops:
  0.0 53.7 %shard_map.100 = bf16[2048,256]{1,0:T(8,128)(2,1)} custom-call(s32[1,2]{1,0:T(1,128)} %near.1, bf16[2048,128]{1,0:T(8,128)(2,1)} %points_in.1, bf16[2048,256]{1,0:T(8,128)(2,1)} %charges_in.1, bf16[2048,256]{1,0:T(8,128)(2,1)} %bases_in.1, s32[1,2048]{1,0:T(1,128)} %order.1, f32[256,256]{1,0:T(8,128)} %lift.1, f32[64,256]{1,0:T(8,128)} %nlift.1, ...), custom_call_target="tpu_custom_call" | custom-call | tf_op jit(solution)/shard_map/pallas_call | solution.py:337
  53.7 2.3 %copy.12 = bf16[2048,256]{1,0:T(8,128)(2,1)} copy(bf16[2048,256]{1,0:T(8,128)(2,1)} %shard_map.100) | data formatting | bytes 2097152
